TPU v7x, 32 devices: a whole 2x2x4 slice. The times are simulated.
32 devices in a mesh: region: 8 (over y, x, core), brick: 4 (over z).
Axes of the slice: x: 2, y: 2, z: 4, core: 2. Of those that a mesh axis runs over, the one named last changes fastest.
Arguments:
- velocity: float32 [3, 128, 64, 256], P(None, 'region', 'brick'), may hold values from -6 to 6
- viscosity: float32 [128, 64, 256], P('region', 'brick'), may hold values from 0.05 to 0.5
- marker_pos: float32 [3, 131072], P(None, ('region', 'brick')), as said below
- marker_force: float32 [3, 131072], P(None, ('region', 'brick')), may hold values from -240 to 240
- slot_lists: int32 [32, 8192], P(('region', 'brick')), may hold values from 0 to 16384, as said below
Outputs:
- predicted: float32 [3, 128, 64, 256], P(None, 'region', 'brick')
Inputs may be any that keep to these rules, and one draw needn't show every extreme that they name: `slot_lists`: each row lists, in increasing order, the indices within its region group's 16384 markers of the markers whose second coordinate lies in that brick's rows, then is padded with 16384; every marker of the group stands in exactly one row, and in every region group one row is full. `marker_pos`: the first coordinate of a marker lies 2 or more cells inside its region group's slab, the third 2 or more cells from the grid's ends, and the second within the rows of the brick whose slot row lists it.
All inputs are finite; a program needn't handle non-finite values.
Results may differ from a plain program's by a relative error of at most 0.00088.
Values sent between devices are 32-bit elements; how exact they have to be, the bound alone decides.
No kernel may reach another device: no remote copies, remote signals or barrier semaphores. Data moves between devices by JAX's collectives and lax.ppermute only.
A program may use at most 192 MiB of HBM per device.

v0:
```python
import jax
import jax.numpy as jnp
from jax import lax
from jax.sharding import PartitionSpec as P


def from_behind(x, axis, by):
    peers = lax.axis_size(axis)
    pairs = [(i, i + by) for i in range(peers) if 0 <= i + by < peers]
    return lax.ppermute(x, axis, pairs)


def extended_2(block, sides, width):
    for axis, dim in sides:
        count = lax.axis_size(axis)
        forward = [(i, i + 1) for i in range(count - 1)]
        backward = [(target, source) for source, target in forward]
        low = lax.ppermute(
            lax.slice_in_dim(block, block.shape[dim] - width, None, axis=dim), axis, forward
        )
        high = lax.ppermute(lax.slice_in_dim(block, 0, width, axis=dim), axis, backward)
        block = jnp.concatenate([low, block, high], axis=dim)
    return block


def kernel_weight(dist):
    return jnp.where(jnp.abs(dist) < 2.0, 0.25 * (1.0 + jnp.cos(0.5 * jnp.pi * dist)), 0.0)


def spread_rows(pos, force, row_low, rows, col_low, cols, depth):
    count = pos.shape[1]
    block = 1024
    x_centre = (col_low + jnp.arange(cols, dtype=jnp.int32)).astype(jnp.float32) + 0.5
    y_centre = (row_low + jnp.arange(rows, dtype=jnp.int32)).astype(jnp.float32) + 0.5
    z_centre = jnp.arange(depth, dtype=jnp.int32).astype(jnp.float32) + 0.5

    def one_block(turn, total):
        start = turn * block
        pos_part = lax.dynamic_slice_in_dim(pos, start, block, 1)
        force_part = lax.dynamic_slice_in_dim(force, start, block, 1)
        weight_x = kernel_weight(x_centre[:, None] - pos_part[0][None, :])
        weight_y = kernel_weight(y_centre[:, None] - pos_part[1][None, :])
        weight_z = kernel_weight(z_centre[None, :] - pos_part[2][:, None])
        factor = (
            force_part[:, None, None, :] * weight_x[None, :, None, :] * weight_y[None, None, :, :]
        )
        factor = factor.reshape(3 * cols * rows, block).astype(jnp.bfloat16)
        return total + jnp.dot(
            factor, weight_z.astype(jnp.bfloat16), preferred_element_type=jnp.float32
        )

    empty = jnp.zeros((3 * cols * rows, depth), jnp.float32)
    total = lax.fori_loop(0, count // block, one_block, empty)
    return total.reshape(3, cols, rows, depth)


def side(array, axis, offset):
    parts = [slice(1, -1), slice(1, -1), slice(1, -1)]
    size = array.shape[array.ndim - 3 + axis]
    parts[axis] = slice(1 + offset, size - 1 + offset)
    if array.ndim == 4:
        return array[:, parts[0], parts[1], parts[2]]
    return array[parts[0], parts[1], parts[2]]


def advance(padded, force_field):
    vel = padded[:3]
    visc = padded[3]
    speed = side(vel, 0, 0)
    visc_mid = side(visc, 0, 0)
    diffusion = jnp.zeros_like(speed)
    advection = jnp.zeros_like(speed)
    for axis in range(3):
        upper = side(vel, axis, 1)
        lower = side(vel, axis, -1)
        visc_up = side(visc, axis, 1)
        visc_dn = side(visc, axis, -1)
        diffusion = (
            diffusion
            + 0.5 * (visc_mid + visc_up) * (upper - speed)
            - 0.5 * (visc_mid + visc_dn) * (speed - lower)
        )
        advection = advection + speed[axis][None] * (upper - lower) * 0.5
    return speed + 0.1 * (diffusion - advection + force_field)


def body(velocity, viscosity, marker_pos, marker_force, slot_lists):
    cols, own_rows, depth = viscosity.shape
    region = lax.axis_index("region")
    brick = lax.axis_index("brick")
    own_slots = slot_lists[0]
    row_low = brick * own_rows - 2
    rows = own_rows + 4
    blank = jnp.zeros((3, own_slots.shape[0]), jnp.float32)
    start = jnp.int32(0)
    pos_piece = lax.all_gather(marker_pos, "brick", axis=1, tiled=True)
    force_piece = lax.all_gather(marker_force, "brick", axis=1, tiled=True)
    length = pos_piece.shape[1]
    inside = ((own_slots >= start) & (own_slots < start + length))[None, :]
    local = jnp.clip(own_slots, 0, length - 1)
    pos = jnp.where(inside, jnp.take(pos_piece, local, axis=1), blank)
    force = jnp.where(inside, jnp.take(force_piece, local, axis=1), blank)
    field = spread_rows(pos, force, row_low, rows, region * cols, cols, depth)
    upper_rim = field[:, :, own_rows + 2 :, :]
    lower_rim = field[:, :, :2, :]
    from_below = from_behind(upper_rim, "brick", 1)
    from_above = from_behind(lower_rim, "brick", -1)
    centre = field[:, :, 2 : own_rows + 2, :]
    centre = centre.at[:, :, :2, :].add(from_below)
    force_field = centre.at[:, :, own_rows - 2 :, :].add(from_above)
    stacked = jnp.concatenate([velocity, viscosity[None]], axis=0)
    extended = extended_2(stacked, (("region", 1), ("brick", 2)), 1)
    padded = jnp.pad(extended, ((0, 0), (0, 0), (0, 0), (1, 1)))
    return advance(padded, force_field)


def solution(mesh):
    placed = (
        P(None, "region", "brick", None),
        P("region", "brick", None),
        P(None, ("region", "brick")),
        P(None, ("region", "brick")),
        P(("region", "brick"), None),
    )
    return jax.shard_map(
        body,
        mesh=mesh,
        in_specs=placed,
        out_specs=P(None, "region", "brick", None),
        check_vma=False,
    )
```

profile of v0, /device:TPU:19, one launch (start us, length us, event | category | flops | bytes accessed | tf_op | source)
XLA Modules:
  0.0 469.4 jit_solution(8026704652510305181)
XLA Ops:
  0.0 0.8 broadcast_clamp_fusion
  0.8 0.9 and_reduce_fusion
  1.7 1.5 copy.10
  3.2 137.8 %all_gather.6 = f32[3,16384]{0,1:T(8,128)} all-gather(f32[3,4096]{0,1:T(8,128)S(1)} %copy.10), channel_id=1, replica_groups=mesh['region'=8,'brick'=4] {'brick'}, dimensions={1}, use_global_device_ids=true | all-gather | bytes 245760 | tf_op jit(solution)/shard_map/all_gather | solution.py:97
  141.0 0.6 copy.11
  141.7 138.8 %all_gather.7 = f32[3,16384]{0,1:T(8,128)} all-gather(f32[3,4096]{0,1:T(8,128)S(1)} %copy.11), channel_id=1, replica_groups=mesh['region'=8,'brick'=4] {'brick'}, dimensions={1}, use_global_device_ids=true | all-gather | bytes 245760 | tf_op jit(solution)/shard_map/all_gather | solution.py:96
  280.4 31.2 %gather_fusion = f32[8192,3]{1,0:T(8,128)} fusion(f32[3,16384]{0,1:T(8,128)} %all_gather.6, s32[8192]{0:T(1024)S(1)} %fusion.44), kind=kCustom, calls=%fused_computation.clone | custom fusion | bytes 229376 | tf_op jit(solution)/shard_map/jit(_take)/gather | solution.py:102
  311.7 31.3 %gather_fusion.1 = f32[8192,3]{1,0:T(8,128)} fusion(f32[3,16384]{0,1:T(8,128)} %all_gather.7, s32[8192]{0:T(1024)S(1)} %fusion.44), kind=kCustom, calls=%fused_computation.1.clone | custom fusion | bytes 229376 | tf_op jit(solution)/shard_map/jit(_take)/gather | solution.py:101
  342.9 8.0 %bitcast_select_fusion = (f32[3,8192]{0,1:T(8,128)}, f32[3,8192]{0,1:T(8,128)}) fusion(f32[8192,3]{1,0:T(8,128)} %gather_fusion.1, pred[8192]{0:T(1024)(128)(4,1)S(1)} %compare_and_fusion, pred[8192]{0:T(1024)(128)(4,1)S(1)} %and_reduce_fusion, f32[8192,3]{1,0:T(8,128)} %gather_fusion), kind=kLoop, calls=%fused_computation.47 | loop fusion | flops 98304 | bytes 409600 | tf_op jit(solution)/shard_map/jit(_where)/select_n | solution.py:101
  350.9 2.8 copy.12
  353.8 2.9 copy.13
  356.6 79.9 %while.16 = (s32[]{:T(128)}, f32[960,256]{1,0:T(8,128)S(1)}, f32[3,8192]{1,0:T(4,128)S(1)}, f32[3,8192]{1,0:T(4,128)S(1)}, s32[]{:T(128)}, /*index=5*/s32[]{:T(1...) while((s32[]{:T(128)}, f32[960,256]{1,0:T(8,128)S(1)}, ...), condition=%wide.region_1.3_spmd.clone, body=%wide.region_0.2_spmd.clone.sunk | while | flops 508179072 | bytes 11381301 | solution.py:53
  357.3 0.4 fusion.56
  357.7 0.6 multiply_convert_fusion.2
  358.3 2.0 convert_element_type.63
  360.3 6.2 %convolution_add_fusion.2 = f32[960,256]{1,0:T(8,128)S(1)} fusion(bf16[960,1024]{1,0:T(8,128)(2,1)} %convert_element_type.63, f32[960,256]{1,0:T(8,128)S(1)} %get-tuple-element.284, f32[1024]{0:T(1024)S(1)} %bitcast.34, f32[256]{0:T(256)S(1)} %convert_add_fusion.8, pred[]{:T(512)S(6)} %compare.35), kind=kOutput, calls=%fused_computation.8.clone.1 | convolution fusion | flops 505905152 | bytes 3937281 | tf_op jit(solution)/shard_map/while/body/eval_jaxpr/dot_general | solution.py:48
  367.7 0.6 multiply_convert_fusion.2
  368.3 2.0 convert_element_type.63
  370.3 6.2 %convolution_add_fusion.2 = f32[960,256]{1,0:T(8,128)S(1)} fusion(bf16[960,1024]{1,0:T(8,128)(2,1)} %convert_element_type.63, f32[960,256]{1,0:T(8,128)S(1)} %get-tuple-element.284, f32[1024]{0:T(1024)S(1)} %bitcast.34, f32[256]{0:T(256)S(1)} %convert_add_fusion.8, pred[]{:T(512)S(6)} %compare.35), kind=kOutput, calls=%fused_computation.8.clone.1 | convolution fusion | flops 505905152 | bytes 3937281 | tf_op jit(solution)/shard_map/while/body/eval_jaxpr/dot_general | solution.py:48
  377.7 0.6 multiply_convert_fusion.2
  378.3 2.0 convert_element_type.63
  380.3 6.3 %convolution_add_fusion.2 = f32[960,256]{1,0:T(8,128)S(1)} fusion(bf16[960,1024]{1,0:T(8,128)(2,1)} %convert_element_type.63, f32[960,256]{1,0:T(8,128)S(1)} %get-tuple-element.284, f32[1024]{0:T(1024)S(1)} %bitcast.34, f32[256]{0:T(256)S(1)} %convert_add_fusion.8, pred[]{:T(512)S(6)} %compare.35), kind=kOutput, calls=%fused_computation.8.clone.1 | convolution fusion | flops 505905152 | bytes 3937281 | tf_op jit(solution)/shard_map/while/body/eval_jaxpr/dot_general | solution.py:48
  387.7 0.6 multiply_convert_fusion.2
  388.3 2.0 convert_element_type.63
  390.3 6.2 %convolution_add_fusion.2 = f32[960,256]{1,0:T(8,128)S(1)} fusion(bf16[960,1024]{1,0:T(8,128)(2,1)} %convert_element_type.63, f32[960,256]{1,0:T(8,128)S(1)} %get-tuple-element.284, f32[1024]{0:T(1024)S(1)} %bitcast.34, f32[256]{0:T(256)S(1)} %convert_add_fusion.8, pred[]{:T(512)S(6)} %compare.35), kind=kOutput, calls=%fused_computation.8.clone.1 | convolution fusion | flops 505905152 | bytes 3937281 | tf_op jit(solution)/shard_map/while/body/eval_jaxpr/dot_general | solution.py:48
  397.7 0.6 multiply_convert_fusion.2
  398.3 2.0 convert_element_type.63
  400.3 6.3 %convolution_add_fusion.2 = f32[960,256]{1,0:T(8,128)S(1)} fusion(bf16[960,1024]{1,0:T(8,128)(2,1)} %convert_element_type.63, f32[960,256]{1,0:T(8,128)S(1)} %get-tuple-element.284, f32[1024]{0:T(1024)S(1)} %bitcast.34, f32[256]{0:T(256)S(1)} %convert_add_fusion.8, pred[]{:T(512)S(6)} %compare.35), kind=kOutput, calls=%fused_computation.8.clone.1 | convolution fusion | flops 505905152 | bytes 3937281 | tf_op jit(solution)/shard_map/while/body/eval_jaxpr/dot_general | solution.py:48
  407.7 0.6 multiply_convert_fusion.2
  408.3 2.0 convert_element_type.63
  410.3 6.3 %convolution_add_fusion.2 = f32[960,256]{1,0:T(8,128)S(1)} fusion(bf16[960,1024]{1,0:T(8,128)(2,1)} %convert_element_type.63, f32[960,256]{1,0:T(8,128)S(1)} %get-tuple-element.284, f32[1024]{0:T(1024)S(1)} %bitcast.34, f32[256]{0:T(256)S(1)} %convert_add_fusion.8, pred[]{:T(512)S(6)} %compare.35), kind=kOutput, calls=%fused_computation.8.clone.1 | convolution fusion | flops 505905152 | bytes 3937281 | tf_op jit(solution)/shard_map/while/body/eval_jaxpr/dot_general | solution.py:48
  417.7 0.6 multiply_convert_fusion.2
  418.3 2.0 convert_element_type.63
  420.3 6.2 %convolution_add_fusion.2 = f32[960,256]{1,0:T(8,128)S(1)} fusion(bf16[960,1024]{1,0:T(8,128)(2,1)} %convert_element_type.63, f32[960,256]{1,0:T(8,128)S(1)} %get-tuple-element.284, f32[1024]{0:T(1024)S(1)} %bitcast.34, f32[256]{0:T(256)S(1)} %convert_add_fusion.8, pred[]{:T(512)S(6)} %compare.35), kind=kOutput, calls=%fused_computation.8.clone.1 | convolution fusion | flops 505905152 | bytes 3937281 | tf_op jit(solution)/shard_map/while/body/eval_jaxpr/dot_general | solution.py:48
  427.7 0.6 multiply_convert_fusion.2
  428.3 2.0 convert_element_type.63
  430.3 6.3 %convolution_add_fusion.2 = f32[960,256]{1,0:T(8,128)S(1)} fusion(bf16[960,1024]{1,0:T(8,128)(2,1)} %convert_element_type.63, f32[960,256]{1,0:T(8,128)S(1)} %get-tuple-element.284, f32[1024]{0:T(1024)S(1)} %bitcast.34, f32[256]{0:T(256)S(1)} %convert_add_fusion.8, pred[]{:T(512)S(6)} %compare.35), kind=kOutput, calls=%fused_computation.8.clone.1 | convolution fusion | flops 505905152 | bytes 3937281 | tf_op jit(solution)/shard_map/while/body/eval_jaxpr/dot_general | solution.py:48
  436.8 4.9 %collective-permute-start.4 = (f32[3,16,2,256]{3,2,1,0:T(2,128)S(1)}, f32[3,16,2,256]{3,2,1,0:T(2,128)S(1)}, u32[]{:S(2)}, u32[]{:S(2)}) collective-permute-start(f32[3,16,2,256]{3,2,1,0:T(2,128)S(1)} %get-tuple-element.214), channel_id=1, source_target_pairs={{0,1},{1,2},{2,3},{4,5},{5,6},{6,7},{8,9},{9,10},{10,11},{12,13},{... | collective-permute-start | bytes 294920 | tf_op jit(solution)/shard_map/ppermute | solution.py:10
  441.7 1.9 collective-permute-start.5
  443.7 5.7 %collective-permute-start = (f32[4,1,16,256]{3,2,1,0:T(8,128)S(1)}, f32[4,1,16,256]{3,2,1,0:T(8,128)S(1)}, u32[]{:S(2)}, u32[]{:S(2)}) collective-permute-start(f32[4,1,16,256]{3,2,1,0:T(8,128)S(1)} %get-tuple-element.215), channel_id=1, source_target_pairs={{0,4},{4,8},{8,12},{12,16},{16,20},{20,24},{24,28},{1,5},{5,9},{9,... | collective-permute-start | bytes 196616 | tf_op jit(solution)/shard_map/ppermute | solution.py:18
  449.3 1.9 collective-permute-start.1
  451.4 4.4 collective-permute-done.1
  455.9 3.6 collective-permute-start.2
  459.6 2.1 collective-permute-start.3
  461.9 2.7 collective-permute-done.3
  464.7 1.3 select_maximum_fusion
  466.1 0.5 fusion.41
  466.6 2.8 multiply_add_fusion
  (117 shorter events, 8.6 us)
Async XLA Ops:
  3.2 137.8 %copy-start.4 = (f32[3,4096]{1,0:T(4,128)S(1)}, f32[3,4096]{1,0:T(4,128)}, u32[]{:S(2)}) copy-start(f32[3,4096]{1,0:T(4,128)} %param.15) | copy-start | bytes 147460
  356.6 0.7 copy-start.2
  360.3 6.3 %copy-start.3 = (f32[3,8192]{1,0:T(4,128)S(1)}, f32[3,8192]{1,0:T(4,128)}, u32[]{:S(2)}) copy-start(f32[3,8192]{1,0:T(4,128)} %copy-done.2) | copy-start | bytes 294916 | tf_op jit(solution)/shard_map/while
  366.6 0.7 copy-start.2
  370.3 6.3 %copy-start.3 = (f32[3,8192]{1,0:T(4,128)S(1)}, f32[3,8192]{1,0:T(4,128)}, u32[]{:S(2)}) copy-start(f32[3,8192]{1,0:T(4,128)} %copy-done.2) | copy-start | bytes 294916 | tf_op jit(solution)/shard_map/while
  376.6 0.7 copy-start.2
  380.3 6.3 %copy-start.3 = (f32[3,8192]{1,0:T(4,128)S(1)}, f32[3,8192]{1,0:T(4,128)}, u32[]{:S(2)}) copy-start(f32[3,8192]{1,0:T(4,128)} %copy-done.2) | copy-start | bytes 294916 | tf_op jit(solution)/shard_map/while
  386.6 0.7 copy-start.2
  390.3 6.3 %copy-start.3 = (f32[3,8192]{1,0:T(4,128)S(1)}, f32[3,8192]{1,0:T(4,128)}, u32[]{:S(2)}) copy-start(f32[3,8192]{1,0:T(4,128)} %copy-done.2) | copy-start | bytes 294916 | tf_op jit(solution)/shard_map/while
  396.6 0.7 copy-start.2
  400.3 6.3 %copy-start.3 = (f32[3,8192]{1,0:T(4,128)S(1)}, f32[3,8192]{1,0:T(4,128)}, u32[]{:S(2)}) copy-start(f32[3,8192]{1,0:T(4,128)} %copy-done.2) | copy-start | bytes 294916 | tf_op jit(solution)/shard_map/while
  406.6 0.7 copy-start.2
  410.3 6.3 %copy-start.3 = (f32[3,8192]{1,0:T(4,128)S(1)}, f32[3,8192]{1,0:T(4,128)}, u32[]{:S(2)}) copy-start(f32[3,8192]{1,0:T(4,128)} %copy-done.2) | copy-start | bytes 294916 | tf_op jit(solution)/shard_map/while
  416.6 0.7 copy-start.2
  420.3 6.3 %copy-start.3 = (f32[3,8192]{1,0:T(4,128)S(1)}, f32[3,8192]{1,0:T(4,128)}, u32[]{:S(2)}) copy-start(f32[3,8192]{1,0:T(4,128)} %copy-done.2) | copy-start | bytes 294916 | tf_op jit(solution)/shard_map/while
  426.6 0.7 copy-start.2
  430.3 6.3 %copy-start.3 = (f32[3,8192]{1,0:T(4,128)S(1)}, f32[3,8192]{1,0:T(4,128)}, u32[]{:S(2)}) copy-start(f32[3,8192]{1,0:T(4,128)} %copy-done.2) | copy-start | bytes 294916 | tf_op jit(solution)/shard_map/while
  436.6 7.1 %copy-start = (f32[3,16,16,256]{3,2,1,0:T(8,128)S(1)}, f32[3,16,16,256]{3,2,1,0:T(8,128)}, u32[]{:S(2)}) copy-start(f32[3,16,16,256]{3,2,1,0:T(8,128)} %param.13) | copy-start | bytes 2359300
  436.6 7.1 %copy-start.1 = (f32[16,16,256]{2,1,0:T(8,128)S(1)}, f32[16,16,256]{2,1,0:T(8,128)}, u32[]{:S(2)}) copy-start(f32[16,16,256]{2,1,0:T(8,128)} %param.14) | copy-start | bytes 786436
  436.8 24.9 %collective-permute-start.4 = (f32[3,16,2,256]{3,2,1,0:T(2,128)S(1)}, f32[3,16,2,256]{3,2,1,0:T(2,128)S(1)}, u32[]{:S(2)}, u32[]{:S(2)}) collective-permute-start(f32[3,16,2,256]{3,2,1,0:T(2,128)S(1)} %get-tuple-element.214), channel_id=1, source_target_pairs={{0,1},{1,2},{2,3},{4,5},{5,6},{6,7},{8,9},{9,10},{10,11},{12,13},{... | collective-permute-start | bytes 294920 | tf_op jit(solution)/shard_map/ppermute | solution.py:10
  441.7 20.1 %collective-permute-start.5 = (f32[3,16,2,256]{3,2,1,0:T(2,128)S(1)}, f32[3,16,2,256]{3,2,1,0:T(2,128)S(1)}, u32[]{:S(2)}, u32[]{:S(2)}) collective-permute-start(f32[3,16,2,256]{3,2,1,0:T(2,128)S(1)} %get-tuple-element.213), channel_id=1, source_target_pairs={{1,0},{2,1},{3,2},{5,4},{6,5},{7,6},{9,8},{10,9},{11,10},{13,12},{... | collective-permute-start | bytes 294920 | tf_op jit(solution)/shard_map/ppermute | solution.py:10
  443.7 7.8 %collective-permute-start = (f32[4,1,16,256]{3,2,1,0:T(8,128)S(1)}, f32[4,1,16,256]{3,2,1,0:T(8,128)S(1)}, u32[]{:S(2)}, u32[]{:S(2)}) collective-permute-start(f32[4,1,16,256]{3,2,1,0:T(8,128)S(1)} %get-tuple-element.215), channel_id=1, source_target_pairs={{0,4},{4,8},{8,12},{12,16},{16,20},{20,24},{24,28},{1,5},{5,9},{9,... | collective-permute-start | bytes 196616 | tf_op jit(solution)/shard_map/ppermute | solution.py:18
  449.3 6.5 %collective-permute-start.1 = (f32[4,1,16,256]{3,2,1,0:T(8,128)S(1)}, f32[4,1,16,256]{3,2,1,0:T(8,128)S(1)}, u32[]{:S(2)}, u32[]{:S(2)}) collective-permute-start(f32[4,1,16,256]{3,2,1,0:T(8,128)S(1)} %get-tuple-element.216), channel_id=1, source_target_pairs={{4,0},{8,4},{12,8},{16,12},{20,16},{24,20},{28,24},{5,1},{9,5},{13... | collective-permute-start | bytes 196616 | tf_op jit(solution)/shard_map/ppermute | solution.py:21
  455.9 6.0 %collective-permute-start.2 = (f32[4,18,1,256]{3,2,1,0:T(1,128)S(1)}, f32[4,18,1,256]{3,2,1,0:T(1,128)S(1)}, u32[]{:S(2)}, u32[]{:S(2)}) collective-permute-start(f32[4,18,1,256]{3,2,1,0:T(1,128)S(1)} %get-tuple-element.211), channel_id=1, source_target_pairs={{0,1},{1,2},{2,3},{4,5},{5,6},{6,7},{8,9},{9,10},{10,11},{12,13},{... | collective-permute-start | bytes 221192 | tf_op jit(solution)/shard_map/ppermute | solution.py:18
  459.6 5.1 %collective-permute-start.3 = (f32[4,18,1,256]{3,2,1,0:T(1,128)S(1)}, f32[4,18,1,256]{3,2,1,0:T(1,128)S(1)}, u32[]{:S(2)}, u32[]{:S(2)}) collective-permute-start(f32[4,18,1,256]{3,2,1,0:T(1,128)S(1)} %get-tuple-element.212), channel_id=1, source_target_pairs={{1,0},{2,1},{3,2},{5,4},{6,5},{7,6},{9,8},{10,9},{11,10},{13,12},{... | collective-permute-start | bytes 221192 | tf_op jit(solution)/shard_map/ppermute | solution.py:21
where the time goes:
time: 470 us; the launch traced here: 469 us
  blocking collectives  277 us (59%)
  local copies, waits for them, and re-layouts  88.8 us (19%)
  matrix products  50 us (11%)
  other arithmetic  25.7 us (5%)
  starting transfers between devices  20.2 us (4%)
  waiting for transfers between devices  7.14 us (2%)
    all_gather x1, blocking collectives, body(): pos_piece = lax.all_gather(marker_pos, 'brick', axis=1, tiled=True)  139 us
    all_gather x1, blocking collectives, body(): force_piece = lax.all_gather(marker_force, 'brick', axis=1, tiled=True)  138 us
    dot_general x8, matrix products, one_block(): jnp.dot(factor, weight_z.astype(jnp.bfloat16), preferred_element_type=jnp...  50 us
    gather x1, local copies, waits for them, and re-layouts, body(): pos = jnp.where(inside, jnp.take(pos_piece, local, axis=1), blank)  31.3 us
    gather x1, local copies, waits for them, and re-layouts, body(): force = jnp.where(inside, jnp.take(force_piece, local, axis=1), blank)  31.2 us
    convert_element_type x8, local copies, waits for them, and re-layouts, one_block(): factor = factor.reshape(3 * cols * rows, block).astype(jnp.bfloat16)  16 us
  transfers between devices with their start and end apart: 6, of which 2 were waited for; matrix products, arithmetic and copies ran while one was open for 0% of the time, Pallas kernels for 0%

commit v1 on v0

--- a/solution.py
+++ b/solution.py
@@ -94,7 +94,14 @@
     blank = jnp.zeros((3, own_slots.shape[0]), jnp.float32)
     start = jnp.int32(0)
     pos_piece = lax.all_gather(marker_pos, "brick", axis=1, tiled=True)
-    force_piece = lax.all_gather(marker_force, "brick", axis=1, tiled=True)
+    n_dev = lax.axis_size("brick")
+    right = [(i_2, (i_2 + 1) % n_dev) for i_2 in range(n_dev)]
+    pieces = [marker_force]
+    for stride in range(1, n_dev):
+        pieces = [lax.ppermute(pieces[0], "brick", right), *pieces]
+    result = jnp.concatenate(pieces, axis=1)
+    shift = (lax.axis_index("brick") + 1) * pieces[-1].shape[1]
+    force_piece = jnp.roll(result, shift, axis=1)
     length = pos_piece.shape[1]
     inside = ((own_slots >= start) & (own_slots < start + length))[None, :]
     local = jnp.clip(own_slots, 0, length - 1)

time: 470 us -> 352 us (0.75)
  blocking collectives: 277 us -> 139 us
  local copies, waits for them, and re-layouts: 88.8 us -> 102 us
  matrix products: 50 us -> 57.3 us
    all_gather x1 -> x0, blocking collectives: 138 us -> none  [body(): force_piece = lax.all_gather(marker_force, 'brick', axis=1, tiled=True)]
    unnamed x10 -> x41, local copies, waits for them, and re-layouts: 7.83 us -> 16.5 us
    dot_general x8, matrix products: 50 us -> 57.3 us  [one_block(): jnp.dot(factor, weight_z.astype(jnp.bfloat16), preferred_element_type=jnp...]
    ppermute x2, waiting for transfers between devices: 7.13 us -> 0.78 us  [extended_2(): lax.ppermute(lax.slice_in_dim(block, 0, width, axis=dim), axis, backward)]
  transfers between devices with their start and end apart: 6 -> 9, of which waited for: 2 -> 2; matrix products, arithmetic and copies ran while one was open for 0% -> 11% of each run, Pallas kernels for 0% -> 0%
where the time goes in v1:
time: 352 us; the launch traced here: 348 us
  blocking collectives  139 us (39%)
  local copies, waits for them, and re-layouts  102 us (29%)
  matrix products  57.3 us (16%)
  other arithmetic  27.2 us (8%)
  starting transfers between devices  18.6 us (5%)
  waiting for transfers between devices  3.82 us (1%)
    all_gather x1, blocking collectives, body(): pos_piece = lax.all_gather(marker_pos, 'brick', axis=1, tiled=True)  139 us
    dot_general x8, matrix products, one_block(): jnp.dot(factor, weight_z.astype(jnp.bfloat16), preferred_element_type=jnp...  57.3 us
    gather x1, local copies, waits for them, and re-layouts, body(): pos = jnp.where(inside, jnp.take(pos_piece, local, axis=1), blank)  31.2 us
    gather x1, local copies, waits for them, and re-layouts, body(): force = jnp.where(inside, jnp.take(force_piece, local, axis=1), blank)  31.1 us
    unnamed x41, local copies, waits for them, and re-layouts  16.5 us
    convert_element_type x8, local copies, waits for them, and re-layouts, one_block(): factor = factor.reshape(3 * cols * rows, block).astype(jnp.bfloat16)  15.7 us
    select_n x1, other arithmetic, body(): pos = jnp.where(inside, jnp.take(pos_piece, local, axis=1), blank)  8.07 us
  transfers between devices with their start and end apart: 9, of which 2 were waited for; matrix products, arithmetic and copies ran while one was open for 11% of the time, Pallas kernels for 0%

profile of v1, /device:TPU:19, one launch (start us, length us, event | category | flops | bytes accessed | tf_op | source)
XLA Modules:
  0.0 347.9 jit_solution(15078338722081781222)
XLA Ops:
  0.0 1.3 collective-permute-start.4
  1.4 1.5 pad_maximum_fusion.17
  2.9 3.9 %collective-permute-start = (f32[4,1,16,256]{3,2,1,0:T(8,128)}, f32[4,1,16,256]{3,2,1,0:T(8,128)S(1)}, u32[]{:S(2)}, u32[]{:S(2)}) collective-permute-start(f32[4,1,16,256]{3,2,1,0:T(8,128)} %get-tuple-element.221), channel_id=1, source_target_pairs={{0,4},{4,8},{8,12},{12,16},{16,20},{20,24},{24,28},{1,5},{5,9},{9,... | collective-permute-start | bytes 196616 | tf_op jit(solution)/shard_map/ppermute | solution.py:18
  6.8 1.9 collective-permute-start.1
  8.7 0.8 broadcast_clamp_fusion
  9.6 2.0 slice_bitcast_fusion.3
  11.8 0.6 copy.19
  12.5 0.8 collective-permute-done.1
  13.3 0.8 pad_maximum_fusion.15
  14.1 2.3 collective-permute-start.2
  16.4 2.9 collective-permute-start.3
  19.4 138.6 %all_gather.3 = f32[3,16384]{0,1:T(8,128)} all-gather(f32[3,4096]{0,1:T(8,128)S(1)} %copy.19), channel_id=1, replica_groups=mesh['region'=8,'brick'=4] {'brick'}, dimensions={1}, use_global_device_ids=true | all-gather | bytes 245760 | tf_op jit(solution)/shard_map/all_gather | solution.py:96
  157.9 31.2 %gather_fusion.1 = f32[8192,3]{1,0:T(8,128)} fusion(f32[3,16384]{0,1:T(8,128)} %all_gather.3, s32[8192]{0:T(1024)S(1)} %fusion.44), kind=kCustom, calls=%fused_computation.1.clone | custom fusion | bytes 229376 | tf_op jit(solution)/shard_map/jit(_take)/gather | solution.py:108
  189.6 1.3 select_maximum_fusion
  191.0 1.5 copy-done.2
  192.5 0.9 slice_bitcast_fusion
  193.4 0.9 constant_dynamic-update-slice_fusion.6
  194.2 0.9 constant_dynamic-update-slice_fusion.5
  195.2 0.9 constant_dynamic-update-slice_fusion.2
  196.0 0.9 constant_dynamic-update-slice_fusion.1
  197.0 5.1 %copy.22 = f32[3,16384]{0,1:T(8,128)} copy(f32[3,16384]{1,0:T(4,128)S(1)} %constant_dynamic-slice_fusion.2) | data formatting | bytes 393216
  202.1 31.1 %gather_fusion = f32[8192,3]{1,0:T(8,128)} fusion(f32[3,16384]{0,1:T(8,128)} %copy.22, s32[8192]{0:T(1024)S(1)} %fusion.44), kind=kCustom, calls=%fused_computation.clone | custom fusion | bytes 229376 | tf_op jit(solution)/shard_map/jit(_take)/gather | solution.py:109
  233.2 8.1 %bitcast_select_fusion = (f32[3,8192]{0,1:T(8,128)}, f32[3,8192]{0,1:T(8,128)}) fusion(f32[8192,3]{1,0:T(8,128)} %gather_fusion.1, pred[8192]{0:T(1024)(128)(4,1)S(1)} %compare_and_fusion, pred[8192]{0:T(1024)(128)(4,1)S(1)} %and_reduce_fusion, f32[8192,3]{1,0:T(8,128)} %gather_fusion), kind=kLoop, calls=%fused_computation.47 | loop fusion | flops 98304 | bytes 409600 | tf_op jit(solution)/shard_map/jit(_where)/select_n | solution.py:108
  241.3 2.8 copy.20
  244.1 2.9 copy.21
  247.0 87.1 %while.16 = (s32[]{:T(128)}, f32[960,256]{1,0:T(8,128)}, f32[3,8192]{1,0:T(4,128)S(1)}, f32[3,8192]{1,0:T(4,128)S(1)}, s32[]{:T(128)}, /*index=5*/s32[]{:T(128)}...) while((s32[]{:T(128)}, f32[960,256]{1,0:T(8,128)}, ...), condition=%wide.region_1.3_spmd.clone, body=%wide.region_0.2_spmd.clone.sunk | while | flops 508179072 | bytes 12167789 | solution.py:53
  248.7 2.0 convert_element_type.63
  250.7 6.9 %convolution_add_fusion.2 = f32[960,256]{1,0:T(8,128)} fusion(bf16[960,1024]{1,0:T(8,128)(2,1)} %convert_element_type.63, f32[960,256]{1,0:T(8,128)} %get-tuple-element.290, f32[1024]{0:T(1024)S(1)} %bitcast.34, f32[256]{0:T(256)S(1)} %convert_add_fusion.8, pred[]{:T(512)S(6)} %compare.36), kind=kOutput, calls=%fused_computation.8.clone.1 | convolution fusion | flops 505905152 | bytes 3937281 | tf_op jit(solution)/shard_map/while/body/eval_jaxpr/dot_general | solution.py:48
  259.4 2.0 convert_element_type.63
  261.4 7.2 %convolution_add_fusion.2 = f32[960,256]{1,0:T(8,128)} fusion(bf16[960,1024]{1,0:T(8,128)(2,1)} %convert_element_type.63, f32[960,256]{1,0:T(8,128)} %get-tuple-element.290, f32[1024]{0:T(1024)S(1)} %bitcast.34, f32[256]{0:T(256)S(1)} %convert_add_fusion.8, pred[]{:T(512)S(6)} %compare.36), kind=kOutput, calls=%fused_computation.8.clone.1 | convolution fusion | flops 505905152 | bytes 3937281 | tf_op jit(solution)/shard_map/while/body/eval_jaxpr/dot_general | solution.py:48
  270.3 2.0 convert_element_type.63
  272.3 7.2 %convolution_add_fusion.2 = f32[960,256]{1,0:T(8,128)} fusion(bf16[960,1024]{1,0:T(8,128)(2,1)} %convert_element_type.63, f32[960,256]{1,0:T(8,128)} %get-tuple-element.290, f32[1024]{0:T(1024)S(1)} %bitcast.34, f32[256]{0:T(256)S(1)} %convert_add_fusion.8, pred[]{:T(512)S(6)} %compare.36), kind=kOutput, calls=%fused_computation.8.clone.1 | convolution fusion | flops 505905152 | bytes 3937281 | tf_op jit(solution)/shard_map/while/body/eval_jaxpr/dot_general | solution.py:48
  281.2 2.0 convert_element_type.63
  283.2 7.2 %convolution_add_fusion.2 = f32[960,256]{1,0:T(8,128)} fusion(bf16[960,1024]{1,0:T(8,128)(2,1)} %convert_element_type.63, f32[960,256]{1,0:T(8,128)} %get-tuple-element.290, f32[1024]{0:T(1024)S(1)} %bitcast.34, f32[256]{0:T(256)S(1)} %convert_add_fusion.8, pred[]{:T(512)S(6)} %compare.36), kind=kOutput, calls=%fused_computation.8.clone.1 | convolution fusion | flops 505905152 | bytes 3937281 | tf_op jit(solution)/shard_map/while/body/eval_jaxpr/dot_general | solution.py:48
  291.5 0.6 multiply_convert_fusion.2
  292.1 2.0 convert_element_type.63
  294.1 7.2 %convolution_add_fusion.2 = f32[960,256]{1,0:T(8,128)} fusion(bf16[960,1024]{1,0:T(8,128)(2,1)} %convert_element_type.63, f32[960,256]{1,0:T(8,128)} %get-tuple-element.290, f32[1024]{0:T(1024)S(1)} %bitcast.34, f32[256]{0:T(256)S(1)} %convert_add_fusion.8, pred[]{:T(512)S(6)} %compare.36), kind=kOutput, calls=%fused_computation.8.clone.1 | convolution fusion | flops 505905152 | bytes 3937281 | tf_op jit(solution)/shard_map/while/body/eval_jaxpr/dot_general | solution.py:48
  303.1 2.0 convert_element_type.63
  305.0 7.2 %convolution_add_fusion.2 = f32[960,256]{1,0:T(8,128)} fusion(bf16[960,1024]{1,0:T(8,128)(2,1)} %convert_element_type.63, f32[960,256]{1,0:T(8,128)} %get-tuple-element.290, f32[1024]{0:T(1024)S(1)} %bitcast.34, f32[256]{0:T(256)S(1)} %convert_add_fusion.8, pred[]{:T(512)S(6)} %compare.36), kind=kOutput, calls=%fused_computation.8.clone.1 | convolution fusion | flops 505905152 | bytes 3937281 | tf_op jit(solution)/shard_map/while/body/eval_jaxpr/dot_general | solution.py:48
  314.0 2.0 convert_element_type.63
  316.0 7.2 %convolution_add_fusion.2 = f32[960,256]{1,0:T(8,128)} fusion(bf16[960,1024]{1,0:T(8,128)(2,1)} %convert_element_type.63, f32[960,256]{1,0:T(8,128)} %get-tuple-element.290, f32[1024]{0:T(1024)S(1)} %bitcast.34, f32[256]{0:T(256)S(1)} %convert_add_fusion.8, pred[]{:T(512)S(6)} %compare.36), kind=kOutput, calls=%fused_computation.8.clone.1 | convolution fusion | flops 505905152 | bytes 3937281 | tf_op jit(solution)/shard_map/while/body/eval_jaxpr/dot_general | solution.py:48
  324.9 2.0 convert_element_type.63
  326.9 7.2 %convolution_add_fusion.2 = f32[960,256]{1,0:T(8,128)} fusion(bf16[960,1024]{1,0:T(8,128)(2,1)} %convert_element_type.63, f32[960,256]{1,0:T(8,128)} %get-tuple-element.290, f32[1024]{0:T(1024)S(1)} %bitcast.34, f32[256]{0:T(256)S(1)} %convert_add_fusion.8, pred[]{:T(512)S(6)} %compare.36), kind=kOutput, calls=%fused_computation.8.clone.1 | convolution fusion | flops 505905152 | bytes 3937281 | tf_op jit(solution)/shard_map/while/body/eval_jaxpr/dot_general | solution.py:48
  334.1 1.4 reshape.182
  335.6 3.3 collective-permute-start.7
  339.5 2.2 collective-permute-start.8
  341.8 3.0 collective-permute-done.8
  345.0 2.8 multiply_add_fusion
  (187 shorter events, 14.7 us)
Async XLA Ops:
  0.0 13.3 %copy-start.4 = (f32[16,16,256]{2,1,0:T(8,128)S(1)}, f32[16,16,256]{2,1,0:T(8,128)}, u32[]{:S(2)}) copy-start(f32[16,16,256]{2,1,0:T(8,128)} %param.14) | copy-start | bytes 786436
  0.0 13.3 %copy-start = (f32[3,16,16,256]{3,2,1,0:T(8,128)S(1)}, f32[3,16,16,256]{3,2,1,0:T(8,128)}, u32[]{:S(2)}) copy-start(f32[3,16,16,256]{3,2,1,0:T(8,128)} %param.13) | copy-start | bytes 2359300
  0.0 11.6 %copy-start.17 = (s32[1,8192]{1,0:T(1,128)S(1)}, s32[1,8192]{1,0:T(1,128)}, u32[]{:S(2)}) copy-start(s32[1,8192]{1,0:T(1,128)} %param.17) | copy-start | bytes 98308
  0.0 11.8 %copy-start.18 = (f32[3,4096]{1,0:T(4,128)S(1)}, f32[3,4096]{1,0:T(4,128)}, u32[]{:S(2)}) copy-start(f32[3,4096]{1,0:T(4,128)} %param.15) | copy-start | bytes 147460
  0.0 12.4 %collective-permute-start.4 = (f32[3,4096]{1,0:T(4,128)}, f32[3,4096]{1,0:T(4,128)}, u32[]{:S(2)}, u32[]{:S(2)}) collective-permute-start(f32[3,4096]{1,0:T(4,128)} %param.16), channel_id=1, source_target_pairs={{0,1},{1,2},{2,3},{3,0},{4,5},{5,6},{6,7},{7,4},{8,9},{9,10},{10,1... | collective-permute-start | bytes 147464 | tf_op jit(solution)/shard_map/ppermute | solution.py:101
  2.9 9.7 %collective-permute-start = (f32[4,1,16,256]{3,2,1,0:T(8,128)}, f32[4,1,16,256]{3,2,1,0:T(8,128)S(1)}, u32[]{:S(2)}, u32[]{:S(2)}) collective-permute-start(f32[4,1,16,256]{3,2,1,0:T(8,128)} %get-tuple-element.221), channel_id=1, source_target_pairs={{0,4},{4,8},{8,12},{12,16},{16,20},{20,24},{24,28},{1,5},{5,9},{9,... | collective-permute-start | bytes 196616 | tf_op jit(solution)/shard_map/ppermute | solution.py:18
  6.8 6.5 %collective-permute-start.1 = (f32[4,1,16,256]{3,2,1,0:T(8,128)S(1)}, f32[4,1,16,256]{3,2,1,0:T(8,128)S(1)}, u32[]{:S(2)}, u32[]{:S(2)}) collective-permute-start(f32[4,1,16,256]{3,2,1,0:T(8,128)S(1)} %get-tuple-element.222), channel_id=1, source_target_pairs={{4,0},{8,4},{12,8},{16,12},{20,16},{24,20},{28,24},{5,1},{9,5},{13... | collective-permute-start | bytes 196616 | tf_op jit(solution)/shard_map/ppermute | solution.py:21
  12.4 176.6 %collective-permute-start.5 = (f32[3,4096]{1,0:T(4,128)}, f32[3,4096]{1,0:T(4,128)}, u32[]{:S(2)}, u32[]{:S(2)}) collective-permute-start(f32[3,4096]{1,0:T(4,128)} %collective-permute-done.4), channel_id=1, source_target_pairs={{0,1},{1,2},{2,3},{3,0},{4,5},{5,6},{6,7},{7,4},{8,9},{9,10},{10,1... | collective-permute-start | bytes 147464 | tf_op jit(solution)/shard_map/ppermute | solution.py:101
  14.1 175.5 %collective-permute-start.2 = (f32[4,18,1,256]{3,2,1,0:T(1,128)}, f32[4,18,1,256]{3,2,1,0:T(1,128)S(1)}, u32[]{:S(2)}, u32[]{:S(2)}) collective-permute-start(f32[4,18,1,256]{3,2,1,0:T(1,128)} %get-tuple-element.217), channel_id=1, source_target_pairs={{0,1},{1,2},{2,3},{4,5},{5,6},{6,7},{8,9},{9,10},{10,11},{12,13},{... | collective-permute-start | bytes 221192 | tf_op jit(solution)/shard_map/ppermute | solution.py:18
  16.4 173.2 %collective-permute-start.3 = (f32[4,18,1,256]{3,2,1,0:T(1,128)}, f32[4,18,1,256]{3,2,1,0:T(1,128)S(1)}, u32[]{:S(2)}, u32[]{:S(2)}) collective-permute-start(f32[4,18,1,256]{3,2,1,0:T(1,128)} %get-tuple-element.218), channel_id=1, source_target_pairs={{1,0},{2,1},{3,2},{5,4},{6,5},{7,6},{9,8},{10,9},{11,10},{13,12},{... | collective-permute-start | bytes 221192 | tf_op jit(solution)/shard_map/ppermute | solution.py:21
  189.1 6.0 %copy-start.16 = (f32[3,4096]{1,0:T(4,128)S(1)}, f32[3,4096]{1,0:T(4,128)}, u32[]{:S(2)}) copy-start(f32[3,4096]{1,0:T(4,128)} %param.16) | copy-start | bytes 147460
  189.1 4.3 %collective-permute-start.6 = (f32[3,4096]{1,0:T(4,128)}, f32[3,4096]{1,0:T(4,128)S(1)}, u32[]{:S(2)}, u32[]{:S(2)}) collective-permute-start(f32[3,4096]{1,0:T(4,128)} %collective-permute-done.5), channel_id=1, source_target_pairs={{0,1},{1,2},{2,3},{3,0},{4,5},{5,6},{6,7},{7,4},{8,9},{9,10},{10,1... | collective-permute-start | bytes 147464 | tf_op jit(solution)/shard_map/ppermute | solution.py:101
  189.6 3.7 %copy-start.10 = (f32[4,18,1,256]{3,2,1,0:T(1,128)}, f32[4,18,1,256]{3,2,1,0:T(1,128)S(1)}, u32[]{:S(2)}) copy-start(f32[4,18,1,256]{3,2,1,0:T(1,128)S(1)} %collective-permute-done.2) | copy-start | bytes 221188
  189.6 3.7 %copy-start.12 = (f32[4,18,1,256]{3,2,1,0:T(1,128)}, f32[4,18,1,256]{3,2,1,0:T(1,128)S(1)}, u32[]{:S(2)}) copy-start(f32[4,18,1,256]{3,2,1,0:T(1,128)S(1)} %collective-permute-done.3) | copy-start | bytes 221188
  191.0 1.5 copy-start.2
  247.0 0.7 copy-start.14
  250.7 6.9 %copy-start.9 = (f32[3,8192]{1,0:T(4,128)S(1)}, f32[3,8192]{1,0:T(4,128)}, u32[]{:S(2)}) copy-start(f32[3,8192]{1,0:T(4,128)} %copy-done.8) | copy-start | bytes 294916 | tf_op jit(solution)/shard_map/while
  250.7 7.0 %copy-start.15 = (f32[3,8192]{1,0:T(4,128)S(1)}, f32[3,8192]{1,0:T(4,128)}, u32[]{:S(2)}) copy-start(f32[3,8192]{1,0:T(4,128)} %copy-done.14) | copy-start | bytes 294916 | tf_op jit(solution)/shard_map/while
  257.7 0.7 copy-start.14
  261.4 7.2 %copy-start.9 = (f32[3,8192]{1,0:T(4,128)S(1)}, f32[3,8192]{1,0:T(4,128)}, u32[]{:S(2)}) copy-start(f32[3,8192]{1,0:T(4,128)} %copy-done.8) | copy-start | bytes 294916 | tf_op jit(solution)/shard_map/while
  261.4 7.2 %copy-start.15 = (f32[3,8192]{1,0:T(4,128)S(1)}, f32[3,8192]{1,0:T(4,128)}, u32[]{:S(2)}) copy-start(f32[3,8192]{1,0:T(4,128)} %copy-done.14) | copy-start | bytes 294916 | tf_op jit(solution)/shard_map/while
  268.6 0.7 copy-start.14
  272.3 7.2 %copy-start.9 = (f32[3,8192]{1,0:T(4,128)S(1)}, f32[3,8192]{1,0:T(4,128)}, u32[]{:S(2)}) copy-start(f32[3,8192]{1,0:T(4,128)} %copy-done.8) | copy-start | bytes 294916 | tf_op jit(solution)/shard_map/while
  272.3 7.2 %copy-start.15 = (f32[3,8192]{1,0:T(4,128)S(1)}, f32[3,8192]{1,0:T(4,128)}, u32[]{:S(2)}) copy-start(f32[3,8192]{1,0:T(4,128)} %copy-done.14) | copy-start | bytes 294916 | tf_op jit(solution)/shard_map/while
  279.5 0.7 copy-start.14
  283.2 7.2 %copy-start.9 = (f32[3,8192]{1,0:T(4,128)S(1)}, f32[3,8192]{1,0:T(4,128)}, u32[]{:S(2)}) copy-start(f32[3,8192]{1,0:T(4,128)} %copy-done.8) | copy-start | bytes 294916 | tf_op jit(solution)/shard_map/while
  283.2 7.2 %copy-start.15 = (f32[3,8192]{1,0:T(4,128)S(1)}, f32[3,8192]{1,0:T(4,128)}, u32[]{:S(2)}) copy-start(f32[3,8192]{1,0:T(4,128)} %copy-done.14) | copy-start | bytes 294916 | tf_op jit(solution)/shard_map/while
  290.4 0.7 copy-start.14
  294.1 7.2 %copy-start.9 = (f32[3,8192]{1,0:T(4,128)S(1)}, f32[3,8192]{1,0:T(4,128)}, u32[]{:S(2)}) copy-start(f32[3,8192]{1,0:T(4,128)} %copy-done.8) | copy-start | bytes 294916 | tf_op jit(solution)/shard_map/while
  294.1 7.2 %copy-start.15 = (f32[3,8192]{1,0:T(4,128)S(1)}, f32[3,8192]{1,0:T(4,128)}, u32[]{:S(2)}) copy-start(f32[3,8192]{1,0:T(4,128)} %copy-done.14) | copy-start | bytes 294916 | tf_op jit(solution)/shard_map/while
  301.3 0.7 copy-start.14
  305.0 7.2 %copy-start.9 = (f32[3,8192]{1,0:T(4,128)S(1)}, f32[3,8192]{1,0:T(4,128)}, u32[]{:S(2)}) copy-start(f32[3,8192]{1,0:T(4,128)} %copy-done.8) | copy-start | bytes 294916 | tf_op jit(solution)/shard_map/while
  305.0 7.2 %copy-start.15 = (f32[3,8192]{1,0:T(4,128)S(1)}, f32[3,8192]{1,0:T(4,128)}, u32[]{:S(2)}) copy-start(f32[3,8192]{1,0:T(4,128)} %copy-done.14) | copy-start | bytes 294916 | tf_op jit(solution)/shard_map/while
  312.2 0.7 copy-start.14
  315.9 7.2 %copy-start.9 = (f32[3,8192]{1,0:T(4,128)S(1)}, f32[3,8192]{1,0:T(4,128)}, u32[]{:S(2)}) copy-start(f32[3,8192]{1,0:T(4,128)} %copy-done.8) | copy-start | bytes 294916 | tf_op jit(solution)/shard_map/while
  315.9 7.2 %copy-start.15 = (f32[3,8192]{1,0:T(4,128)S(1)}, f32[3,8192]{1,0:T(4,128)}, u32[]{:S(2)}) copy-start(f32[3,8192]{1,0:T(4,128)} %copy-done.14) | copy-start | bytes 294916 | tf_op jit(solution)/shard_map/while
  323.1 0.7 copy-start.14
  326.9 7.2 %copy-start.9 = (f32[3,8192]{1,0:T(4,128)S(1)}, f32[3,8192]{1,0:T(4,128)}, u32[]{:S(2)}) copy-start(f32[3,8192]{1,0:T(4,128)} %copy-done.8) | copy-start | bytes 294916 | tf_op jit(solution)/shard_map/while
  326.9 7.2 %copy-start.15 = (f32[3,8192]{1,0:T(4,128)S(1)}, f32[3,8192]{1,0:T(4,128)}, u32[]{:S(2)}) copy-start(f32[3,8192]{1,0:T(4,128)} %copy-done.14) | copy-start | bytes 294916 | tf_op jit(solution)/shard_map/while
  334.1 4.9 %copy-start.1 = (f32[18,18,258]{2,1,0:T(8,128)S(1)}, f32[18,18,258]{2,1,0:T(8,128)}, u32[]{:S(2)}) copy-start(f32[18,18,258]{2,1,0:T(8,128)} %slice_bitcast_fusion) | copy-start | bytes 1003108
  335.5 9.5 %copy-start.3 = (f32[4,18,18,258]{3,2,1,0:T(8,128)S(1)}, f32[4,18,18,258]{3,2,1,0:T(8,128)}, u32[]{:S(2)}) copy-start(f32[4,18,18,258]{3,2,1,0:T(8,128)} %copy-done.2) | copy-start | bytes 4012420
  335.5 9.5 %copy-start.5 = (f32[16,16,256]{2,1,0:T(8,128)S(1)}, f32[16,16,256]{2,1,0:T(8,128)}, u32[]{:S(2)}) copy-start(f32[16,16,256]{2,1,0:T(8,128)} %get-tuple-element.223) | copy-start | bytes 786436
  335.5 9.5 %copy-start.6 = (f32[16,16,256]{2,1,0:T(8,128)S(1)}, f32[16,16,256]{2,1,0:T(8,128)}, u32[]{:S(2)}) copy-start(f32[16,16,256]{2,1,0:T(8,128)} %get-tuple-element.224) | copy-start | bytes 786436
  335.5 9.5 %copy-start.7 = (f32[16,16,256]{2,1,0:T(8,128)S(1)}, f32[16,16,256]{2,1,0:T(8,128)}, u32[]{:S(2)}) copy-start(f32[16,16,256]{2,1,0:T(8,128)} %get-tuple-element.225) | copy-start | bytes 786436
  335.6 9.5 %copy-start.11 = (f32[4,18,1,256]{3,2,1,0:T(1,128)S(1)}, f32[4,18,1,256]{3,2,1,0:T(1,128)}, u32[]{:S(2)}) copy-start(f32[4,18,1,256]{3,2,1,0:T(1,128)} %copy-done.10) | copy-start | bytes 221188
  335.6 9.5 %copy-start.13 = (f32[4,18,1,256]{3,2,1,0:T(1,128)S(1)}, f32[4,18,1,256]{3,2,1,0:T(1,128)}, u32[]{:S(2)}) copy-start(f32[4,18,1,256]{3,2,1,0:T(1,128)} %copy-done.12) | copy-start | bytes 221188
  335.6 6.2 %collective-permute-start.7 = (f32[3,16,2,256]{3,2,1,0:T(2,128)S(1)}, f32[3,16,2,256]{3,2,1,0:T(2,128)S(1)}, u32[]{:S(2)}, u32[]{:S(2)}) collective-permute-start(f32[3,16,2,256]{3,2,1,0:T(2,128)S(1)} %get-tuple-element.220), channel_id=1, source_target_pairs={{0,1},{1,2},{2,3},{4,5},{5,6},{6,7},{8,9},{9,10},{10,11},{12,13},{... | collective-permute-start | bytes 294920 | tf_op jit(solution)/shard_map/ppermute | solution.py:10
  339.5 5.4 %collective-permute-start.8 = (f32[3,16,2,256]{3,2,1,0:T(2,128)S(1)}, f32[3,16,2,256]{3,2,1,0:T(2,128)S(1)}, u32[]{:S(2)}, u32[]{:S(2)}) collective-permute-start(f32[3,16,2,256]{3,2,1,0:T(2,128)S(1)} %get-tuple-element.219), channel_id=1, source_target_pairs={{1,0},{2,1},{3,2},{5,4},{6,5},{7,6},{9,8},{10,9},{11,10},{13,12},{... | collective-permute-start | bytes 294920 | tf_op jit(solution)/shard_map/ppermute | solution.py:10
  (8 other events, 5.3 us)
